TPU v7x, 32 devices: a whole 2x2x4 slice. The times are simulated.
32 devices in a mesh: rep: 2 (over y), step: 4 (over z), patch: 4 (over x, core).
Axes of the slice: x: 2, y: 2, z: 4, core: 2. Of those that a mesh axis runs over, the one named last changes fastest.
Arguments:
- latent_old: float32 [8, 1024, 64], P(('rep', 'step'), 'patch'), parts along dimension 0, may hold values from -6 to 6
- noise_start: float32 [2048, 64], P(('rep', 'patch')), parts along dimension 0, may hold values from -6 to 6
- step_index: int32 [8], P(('rep', 'step')), parts along dimension 0, may hold values from 0 to 998
- sigma_table: float32 [1000], replicated, may hold values from 0.02 to 1
- mod_weight: bfloat16 [256, 9216], replicated, may hold values from -0.375 to 0.375
- embed_weight: bfloat16 [64, 3072], replicated, may hold values from -0.75 to 0.75
- embed_bias: float32 [3072], replicated, may hold values from -3 to 3
- query_weight: bfloat16 [3072, 1536], P('step'), may hold values from -0.109375 to 0.109375
- query_gain: float32 [128], replicated, may hold values from 0.1 to 1.9
- stale_keys: bfloat16 [8, 1280, 1536], P(('rep', 'step'), 'patch'), parts along dimension 0, may hold values from -640 to 640
- stale_values: bfloat16 [8, 1280, 1536], P(('rep', 'step'), 'patch'), parts along dimension 0, may hold values from -6 to 6
- out_weight: bfloat16 [3072, 1536], P('step'), may hold values from -0.3125 to 0.3125
- final_weight: bfloat16 [3072, 64], replicated, may hold values from -0.109375 to 0.109375
Outputs:
- latent_new: float32 [8, 1024, 64], P(('rep', 'step'), 'patch'), parts along dimension 0
There are 2 independent parts, one for each index of `rep`. A program takes and returns all parts, laid end to end along the dimension named above; an argument that names none is the same for every part. Nothing has to cross between parts.
All inputs are finite; a program needn't handle non-finite values.
Results may differ from a plain program's by a relative error of at most 0.012.
The roundings to bfloat16 on the way count: a program that leaves them out, or rounds other values in their place, can miss the bound.
Values may be sent and summed in bfloat16 or wider, within the bound.
A program may use at most 128 MiB of HBM per device.

v0:
```python
import math
import jax
import jax.numpy as jnp
from jax import lax
from jax.sharding import PartitionSpec as P

D = 3072
HEAD = 128
FREQ = 256
HEADS = 12
epsilon = 1e-06


def entering(shard, axis, join, neutral):
    place = lax.axis_index(axis)
    gathered = lax.all_gather(shard.astype(jnp.bfloat16), axis)
    state = jnp.zeros_like(shard) + jnp.asarray(neutral, shard.dtype)

    def one(hop, state):
        return join(state, lax.dynamic_index_in_dim(gathered, hop, 0, False).astype(shard.dtype))

    return lax.fori_loop(0, place, one, state)


def layer_norm(values_in):
    row_mean = jnp.mean(values_in, axis=-1, keepdims=True)
    centered = values_in - row_mean
    row_var = jnp.mean(centered * centered, axis=-1, keepdims=True)
    return centered * lax.rsqrt(row_var + epsilon)


def time_embed(sigma_now):
    half_count = FREQ // 2
    frequency = jnp.exp(
        -math.log(10000.0) * jnp.arange(half_count).astype(jnp.float32) / half_count
    )
    angles = 1000.0 * sigma_now * frequency
    return jnp.concatenate([jnp.cos(angles), jnp.sin(angles)])


def project_back(attended, weight_rows):
    return lax.dot_general(
        attended, weight_rows, (((1,), (1,)), ((), ())), preferred_element_type=jnp.float32
    )


def norm_queries(raw_queries, query_gain):
    token_count = raw_queries.shape[0]
    head_count = raw_queries.shape[1] // HEAD
    queries = raw_queries.reshape(token_count, head_count, HEAD)
    queries = (
        queries
        * lax.rsqrt(jnp.mean(queries * queries, axis=-1, keepdims=True) + epsilon)
        * query_gain
    )
    return queries.astype(jnp.bfloat16)


def empty_state(queries):
    token_count = queries.shape[0]
    head_count = queries.shape[1]
    return (
        jnp.full((head_count, token_count), -jnp.inf, jnp.float32),
        jnp.zeros((head_count, token_count), jnp.float32),
        jnp.zeros((head_count, token_count, HEAD), jnp.float32),
    )


def attend_block(queries, state_tuple, key_piece, value_piece):
    head_count = queries.shape[1]
    row_count = key_piece.shape[0]
    key_split = key_piece.reshape(row_count, head_count, HEAD)
    value_split = value_piece.reshape(row_count, head_count, HEAD)
    run_peak, run_total, run_sum = state_tuple
    scores = jnp.einsum(
        "qhd,khd->hqk", queries, key_split, preferred_element_type=jnp.float32
    ) / math.sqrt(HEAD)
    new_peak = jnp.max(scores, axis=-1)
    rescale = jnp.exp(run_peak - new_peak)
    exp_weights = jnp.exp(scores - new_peak[..., None])
    run_total = run_total * rescale + jnp.sum(exp_weights, axis=-1)
    run_sum = run_sum * rescale[..., None] + jnp.einsum(
        "hqk,khd->hqd",
        exp_weights.astype(jnp.bfloat16),
        value_split,
        preferred_element_type=jnp.float32,
    )
    return (new_peak, run_total, run_sum)


def finish_heads(state_tuple):
    final_peak, final_total, final_sum = state_tuple
    blended = final_sum / final_total[..., None]
    token_count = blended.shape[1]
    return jnp.transpose(blended, (1, 0, 2)).reshape(token_count, -1).astype(jnp.bfloat16)


def per_device(
    latent_old,
    noise_start,
    step_index,
    sigma_table,
    mod_weight,
    embed_weight,
    embed_bias,
    query_weight,
    query_gain,
    stale_keys,
    stale_values,
    out_weight,
    final_weight,
):
    step_slot = step_index[0]
    table_slots = jnp.arange(sigma_table.shape[0])
    sigma_now = jnp.sum(jnp.where(table_slots == step_slot, sigma_table, 0.0))
    sigma_next = jnp.sum(jnp.where(table_slots == step_slot + 1, sigma_table, 0.0))
    embedded = jax.nn.silu(time_embed(sigma_now)).astype(jnp.bfloat16)
    modulate = jnp.dot(embedded[None, :], mod_weight, preferred_element_type=jnp.float32)[0]
    width = D
    shift_vec = modulate[:width]
    scale_vec = modulate[width : 2 * width]
    gate_vec = modulate[2 * width :]
    latent = latent_old[0]
    token_count = latent.shape[0]
    hidden = (
        jnp.dot(latent.astype(jnp.bfloat16), embed_weight, preferred_element_type=jnp.float32)
        + embed_bias
    )
    normed = (layer_norm(hidden) * (1.0 + scale_vec) + shift_vec).astype(jnp.bfloat16)
    patch_count = lax.axis_size("patch")
    group_width = HEADS // patch_count * HEAD
    patch_slot = lax.axis_index("patch")
    query_columns = lax.dynamic_slice_in_dim(query_weight, patch_slot * group_width, group_width, 1)
    normed_every = lax.all_gather(normed, "patch", axis=0, tiled=True)
    raw_every = jnp.dot(
        normed_every,
        lax.all_gather(query_columns, "step", axis=0, tiled=True),
        preferred_element_type=jnp.float32,
    )
    queries_every = norm_queries(raw_every, query_gain)
    keys_group, values_group = (
        lax.all_to_all(stale_keys[0], "patch", split_axis=1, concat_axis=0, tiled=True),
        lax.all_to_all(stale_values[0], "patch", split_axis=1, concat_axis=0, tiled=True),
    )
    state_every = attend_block(queries_every, empty_state(queries_every), keys_group, values_group)
    attended_every = finish_heads(state_every)
    attended = lax.all_to_all(attended_every, "patch", split_axis=0, concat_axis=1, tiled=True)
    branch = project_back(attended, lax.all_gather(out_weight, "step", axis=0, tiled=True))
    mixed = hidden + gate_vec * branch
    velocity = jnp.dot(
        layer_norm(mixed).astype(jnp.bfloat16), final_weight, preferred_element_type=jnp.float32
    )
    drift_term = velocity * (sigma_next - sigma_now)
    flat_term = drift_term.reshape(-1, 128)

    def add_terms(earlier, later):
        return earlier + later

    prefix = entering(flat_term, "step", add_terms, jnp.zeros_like(flat_term))
    result = noise_start + (prefix + flat_term).reshape(token_count, -1)
    return result[None]


def solution(mesh):
    placed = (
        P(("rep", "step"), "patch", None),
        P(("rep", "patch"), None),
        P(("rep", "step")),
        P(),
        P(),
        P(),
        P(),
        P("step", None),
        P(),
        P(("rep", "step"), "patch", None),
        P(("rep", "step"), "patch", None),
        P("step", None),
        P(),
    )
    return jax.shard_map(
        per_device,
        mesh=mesh,
        in_specs=placed,
        out_specs=P(("rep", "step"), "patch", None),
        check_vma=False,
    )
```

profile of v0, /device:TPU:0, one launch (start us, length us, event | category | flops | bytes accessed | tf_op | source)
XLA Modules:
  0.0 305.8 jit_solution(14107807590935253234)
XLA Ops:
  17.8 2.7 all_to_all.36
  20.5 2.3 copy.38
  22.8 4.2 %all-to-all-start = ((bf16[320,4,384]{2,0,1:T(8,128)(2,1)}), bf16[320,4,384]{2,0,1:T(8,128)(2,1)}, u32[]{:S(2)}, u32[]{:S(2)}) async-start(bf16[320,4,384]{2,0,1:T(8,128)(2,1)} %copy.38), calls=%async_computation | async-start | bytes 1966080 | tf_op jit(solution)/shard_map/all_to_all | solution.py:142
  27.0 2.7 all_to_all.39
  29.7 2.3 copy.41
  32.0 9.4 %all-to-all-done = bf16[320,4,384]{2,0,1:T(8,128)(2,1)} async-done(((bf16[320,4,384]{2,0,1:T(8,128)(2,1)}), bf16[320,4,384]{2,0,1:T(8,128)(2,1)}, u32[]{:S(2)}, u32[]{:S(2)}) %all-to-all-start) | async-done | bytes 983072 | tf_op jit(solution)/shard_map/all_to_all | solution.py:142
  41.5 4.4 %all-to-all-start.1 = ((bf16[320,4,384]{2,0,1:T(8,128)(2,1)}), bf16[320,4,384]{2,0,1:T(8,128)(2,1)}, u32[]{:S(2)}, u32[]{:S(2)}) async-start(bf16[320,4,384]{2,0,1:T(8,128)(2,1)} %copy.41), calls=%async_computation.1 | async-start | bytes 1966080 | tf_op jit(solution)/shard_map/all_to_all | solution.py:143
  45.9 3.7 %reshape.109 = bf16[1280,3,128]{2,1,0:T(4,128)(2,1)} reshape(bf16[4,320,384]{2,1,0:T(8,128)(2,1)} %bitcast.5) | data formatting | bytes 1966080 | tf_op jit(solution)/shard_map/reshape | solution.py:72
  49.6 9.9 %all-to-all-done.1 = bf16[320,4,384]{2,0,1:T(8,128)(2,1)} async-done(((bf16[320,4,384]{2,0,1:T(8,128)(2,1)}), bf16[320,4,384]{2,0,1:T(8,128)(2,1)}, u32[]{:S(2)}, u32[]{:S(2)}) %all-to-all-start.1) | async-done | bytes 983072 | tf_op jit(solution)/shard_map/all_to_all | solution.py:143
  59.5 3.7 %reshape.110 = bf16[1280,3,128]{2,1,0:T(4,128)(2,1)} reshape(bf16[4,320,384]{2,1,0:T(8,128)(2,1)} %bitcast.7) | data formatting | bytes 1966080 | tf_op jit(solution)/shard_map/reshape | solution.py:73
  63.2 45.6 %all-gather.4.cloned.1.call-done = bf16[1024,3072]{1,0:T(8,128)(2,1)} async-done(((bf16[256,3072]{1,0:T(8,128)(2,1)}), bf16[1024,3072]{1,0:T(8,128)(2,1)}) %all-gather.4.cloned.1.call-update) | async-done | bytes 6291472 | tf_op jit(solution)/shard_map/all_gather | solution.py:134
  108.7 7.3 %fusion.31 = f32[1024,384]{0,1:T(8,128)} fusion(bf16[1024,3072]{1,0:T(8,128)(2,1)} %all-gather.4.cloned.1.call-done, bf16[3072,384]{1,0:T(8,128)(2,1)} %all-gather.6.cloned.1.call-done), kind=kOutput, calls=%fused_computation.57 | convolution fusion | flops 2415919104 | bytes 10223616 | tf_op jit(solution)/shard_map/dot_general | solution.py:135
  116.0 3.3 %copy.37 = f32[1024,3,128]{2,0,1:T(8,128)} copy(f32[1024,3,128]{0,2,1:T(8,128)} %bitcast.44) | data formatting | bytes 3145728 | tf_op jit(solution)/shard_map/reshape | solution.py:50
  121.1 4.4 %multiply_reduce_fusion = (f32[3,1024]{1,0:T(4,128)S(1)}, f32[3,1024,1280]{2,1,0:T(8,128)S(1)}) fusion(bf16[1280,3,128]{2,1,0:T(4,128)(2,1)} %reshape.109, f32[1024,3,128]{2,0,1:T(8,128)} %copy.37, f32[128]{0:T(128)S(1)} %copy-done.6, f32[1024,3]{0,1:T(4,128)S(1)} %add_rsqrt_fusion), kind=kOutput, calls=%fused_computation.2 | convolution fusion | flops 1015673856 | bytes 18309632 | tf_op jit(solution)/shard_map/qhd,khd->hqk/dot_general | solution.py:75
  125.6 3.3 %fusion = f32[3,1024]{1,0:T(4,128)S(1)} fusion(f32[3,1024,1280]{2,1,0:T(8,128)S(1)} %get-tuple-element.45, f32[3,1024]{1,0:T(4,128)S(1)} %get-tuple-element.44), kind=kLoop, calls=%fused_computation.3 | loop fusion | flops 11793408 | bytes 15753216 | tf_op jit(solution)/shard_map/reduce_sum | solution.py:81
  128.9 4.5 %fusion.9 = bf16[1024,3,128]{2,0,1:T(8,128)(2,1)} fusion(f32[3,1024,1280]{2,1,0:T(8,128)S(1)} %get-tuple-element.45, f32[3,1024]{1,0:T(4,128)S(1)} %get-tuple-element.44, bf16[1280,3,128]{2,1,0:T(4,128)(2,1)S(1)} %copy-done.3, f32[1024,3]{0,1:T(4,128)S(1)} %bitcast_add_fusion.1, f32[1024,3]{0,1:T(4,128)S(1)} %multiply_bitcast_fusion), kind=kOutput, calls=%fused_computation.18 | convolution fusion | flops 1019609088 | bytes 17534976 | tf_op jit(solution)/shard_map/hqk,khd->hqd/dot_general | solution.py:82
  133.4 2.3 copy.44
  135.7 2.6 convert_element_type.59
  138.3 2.1 copy.45
  140.5 4.2 %all-to-all-start.2 = ((bf16[4,256,384]{1,2,0:T(8,128)(2,1)}), bf16[4,256,384]{1,2,0:T(8,128)(2,1)}, u32[]{:S(2)}, u32[]{:S(2)}) async-start(bf16[4,256,384]{1,2,0:T(8,128)(2,1)} %copy.45), calls=%async_computation.2 | async-start | bytes 1572864 | tf_op jit(solution)/shard_map/all_to_all | solution.py:147
  146.1 10.3 %all-to-all-done.2 = bf16[4,256,384]{1,2,0:T(8,128)(2,1)} async-done(((bf16[4,256,384]{1,2,0:T(8,128)(2,1)}), bf16[4,256,384]{1,2,0:T(8,128)(2,1)}, u32[]{:S(2)}, u32[]{:S(2)}) %all-to-all-start.2) | async-done | bytes 786464 | tf_op jit(solution)/shard_map/all_to_all | solution.py:147
  156.4 120.7 %all-gather.8.cloned.1.call-done = bf16[3072,1536]{1,0:T(8,128)(2,1)} async-done(((bf16[768,1536]{1,0:T(8,128)(2,1)}), bf16[3072,1536]{1,0:T(8,128)(2,1)}) %all-gather.8.cloned.1.call-update) | async-done | bytes 9437200 | tf_op jit(solution)/shard_map/all_gather | solution.py:148
  277.1 5.6 %fusion.28 = (f32[256]{0:T(256)S(1)}, f32[256,3072]{1,0:T(8,128)S(1)}) fusion(f32[256,3072]{1,0:T(8,128)S(1)} %get-tuple-element.43, bf16[256,1536]{0,1:T(8,128)(2,1)} %bitcast.11, bf16[3072,1536]{1,0:T(8,128)(2,1)} %all-gather.8.cloned.1.call-done, f32[3072]{0:T(1024)S(1)} %get-tuple-element.39), kind=kOutput, calls=%fused_computation.54 | convolution fusion | flops 2418278144 | bytes 16528384 | tf_op jit(solution)/shard_map/dot_general | solution.py:42
  284.7 13.6 %all_gather.16 = bf16[4,128,128]{2,1,0:T(8,128)(2,1)S(1)} all-gather(bf16[1,128,128]{2,1,0:T(8,128)(2,1)S(1)} %convert_element_type.62), channel_id=1, replica_groups=mesh['rep'=2,'step'=4,'patch'=4] {'step'}, dimensions={0}, use_global_device_ids=true | all-gather | bytes 163840 | tf_op jit(solution)/shard_map/all_gather | solution.py:16
  (52 shorter events, 14.6 us)
Async XLA Ops:
  6.5 1.7 copy-start
  6.5 56.6 %all-gather.6.cloned.1.call-start = ((), (), s32[]{:S(2)}) async-start(), calls=%async_computation.4 | async-start | bytes 2949120 | tf_op jit(solution)/shard_map/all_gather | solution.py:137
  9.1 99.6 %all-gather.4.cloned.1.call-start = ((), (), s32[]{:S(2)}) async-start(), calls=%async_computation.3 | async-start | bytes 7864320 | tf_op jit(solution)/shard_map/all_gather | solution.py:134
  11.9 2.5 copy-start.2
  17.0 260.1 %all-gather.8.cloned.1.call-start = ((), (), s32[]{:S(2)}) async-start(), calls=%async_computation.5 | async-start | bytes 11796480 | tf_op jit(solution)/shard_map/all_gather | solution.py:148
  22.8 18.6 %all-to-all-start = ((bf16[320,4,384]{2,0,1:T(8,128)(2,1)}), bf16[320,4,384]{2,0,1:T(8,128)(2,1)}, u32[]{:S(2)}, u32[]{:S(2)}) async-start(bf16[320,4,384]{2,0,1:T(8,128)(2,1)} %copy.38), calls=%async_computation | async-start | bytes 1966080 | tf_op jit(solution)/shard_map/all_to_all | solution.py:142
  41.5 18.0 %all-to-all-start.1 = ((bf16[320,4,384]{2,0,1:T(8,128)(2,1)}), bf16[320,4,384]{2,0,1:T(8,128)(2,1)}, u32[]{:S(2)}, u32[]{:S(2)}) async-start(bf16[320,4,384]{2,0,1:T(8,128)(2,1)} %copy.41), calls=%async_computation.1 | async-start | bytes 1966080 | tf_op jit(solution)/shard_map/all_to_all | solution.py:143
  116.0 5.1 %copy-start.6 = (f32[128]{0:T(128)S(1)}, f32[128]{0:T(128)}, u32[]{:S(2)}) copy-start(f32[128]{0:T(128)} %param.23) | copy-start | bytes 1540
  125.5 3.4 %copy-start.3 = (bf16[1280,3,128]{2,1,0:T(4,128)(2,1)S(1)}, bf16[1280,3,128]{2,1,0:T(4,128)(2,1)}, u32[]{:S(2)}) copy-start(bf16[1280,3,128]{2,1,0:T(4,128)(2,1)} %reshape.110) | copy-start | bytes 2949124
  133.4 12.5 %copy-start.5 = (f32[256,64]{0,1:T(8,128)S(1)}, f32[256,64]{0,1:T(8,128)}, u32[]{:S(2)}) copy-start(f32[256,64]{0,1:T(8,128)} %param.16) | copy-start | bytes 196612
  140.5 15.9 %all-to-all-start.2 = ((bf16[4,256,384]{1,2,0:T(8,128)(2,1)}), bf16[4,256,384]{1,2,0:T(8,128)(2,1)}, u32[]{:S(2)}, u32[]{:S(2)}) async-start(bf16[4,256,384]{1,2,0:T(8,128)(2,1)} %copy.45), calls=%async_computation.2 | async-start | bytes 1572864 | tf_op jit(solution)/shard_map/all_to_all | solution.py:147
  282.7 1.0 copy-start.4
  283.2 16.1 %copy-start.1 = (bf16[768,1536]{1,0:T(8,128)(2,1)S(1)}, bf16[768,1536]{1,0:T(8,128)(2,1)}, u32[]{:S(2)}) copy-start(bf16[768,1536]{1,0:T(8,128)(2,1)} %param.22) | copy-start | bytes 7077892
Sparse Core Ops, SparseCore 0:
  9.2 52.7 all-gather.5
  63.6 45.1 all-gather.3
  110.3 166.7 all-gather.7
where the time goes:
time: 307 us; the launch traced here: 306 us
  waiting for transfers between devices  197 us (64%)
  local copies, waits for them, and re-layouts  32.3 us (11%)
  matrix products  25 us (8%)
  between operations  15.9 us (5%)
  blocking collectives  13.6 us (4%)
  starting transfers between devices  12.9 us (4%)
  other arithmetic  9.39 us (3%)
    all_gather x1, waiting for transfers between devices, per_device(): lax.all_gather(out_weight, 'step', axis=0, tiled=True)  121 us
    all_gather x1, waiting for transfers between devices, per_device(): normed_every = lax.all_gather(normed, 'patch', axis=0, tiled=True)  45.6 us
    all_gather x1, blocking collectives, entering(): gathered = lax.all_gather(shard.astype(jnp.bfloat16), axis)  13.6 us
    all_to_all x1, waiting for transfers between devices, per_device(): lax.all_to_all(attended_every, 'patch', split_axis=0, concat_axis=1, tile...  10.3 us
    all_to_all x1, waiting for transfers between devices, per_device(): lax.all_to_all(stale_values[0], 'patch', split_axis=1, concat_axis=0, til...  9.9 us
    all_to_all x1, waiting for transfers between devices, per_device(): lax.all_to_all(stale_keys[0], 'patch', split_axis=1, concat_axis=0, tiled...  9.43 us
    dot_general x1, matrix products, per_device(): jnp.dot(normed_every, lax.all_gather(query_columns, 'step', axis=0, tiled...  7.27 us
    convert_element_type x3, local copies, waits for them, and re-layouts, finish_heads(): jnp.transpose(blended, (1, 0, 2)).reshape(token_count, -1)  7.09 us
  transfers between devices with their start and end apart: 6, of which 5 were waited for; matrix products, arithmetic and copies ran while one was open for 16% of the time, Pallas kernels for 0%

commit v1 on v0

--- a/solution.py
+++ b/solution.py
@@ -3,12 +3,28 @@
 import jax.numpy as jnp
 from jax import lax
 from jax.sharding import PartitionSpec as P
+from jax.lax import axis_index, axis_size, ppermute
 
 D = 3072
 HEAD = 128
 FREQ = 256
 HEADS = 12
 epsilon = 1e-06
+
+
+def define_the_core(array_here):
+    comm_axis = "patch"
+    workers = axis_size(comm_axis)
+    parts_out = [(u - 1, u) for u in range(1, workers)] + [(workers - 1, 0)]
+    a_next = array_here
+    windows = [a_next]
+    for _ in range(workers - 1):
+        a_next = ppermute(a_next, comm_axis, perm=parts_out)
+        windows += [a_next]
+    val2 = jnp.concatenate([*reversed(windows)], axis=0)
+    mixed_arr = axis_index(comm_axis)
+    local_now = jnp.roll(val2, (mixed_arr + 1) * a_next.shape[0], 0)
+    return local_now
 
 
 def entering(shard, axis, join, neutral):
@@ -131,7 +147,7 @@
     group_width = HEADS // patch_count * HEAD
     patch_slot = lax.axis_index("patch")
     query_columns = lax.dynamic_slice_in_dim(query_weight, patch_slot * group_width, group_width, 1)
-    normed_every = lax.all_gather(normed, "patch", axis=0, tiled=True)
+    normed_every = define_the_core(normed)
     raw_every = jnp.dot(
         normed_every,
         lax.all_gather(query_columns, "step", axis=0, tiled=True),

time: 307 us -> 259 us (0.84)
  waiting for transfers between devices: 197 us -> 128 us
  local copies, waits for them, and re-layouts: 32.3 us -> 46.6 us
    all_gather x1, waiting for transfers between devices: 121 us -> 53.6 us  [per_device(): lax.all_gather(out_weight, 'step', axis=0, tiled=True)]
    all_gather x1 -> x0, waiting for transfers between devices: 45.6 us -> none  [per_device(): normed_every = lax.all_gather(normed, 'patch', axis=0, tiled=True)]
    ppermute x0 -> x3, waiting for transfers between devices: none -> 40 us  [define_the_core(): a_next = ppermute(a_next, comm_axis, perm=parts_out)]
    unnamed x15 -> x33, local copies, waits for them, and re-layouts: 2.46 us -> 16.8 us
    all_to_all x1, waiting for transfers between devices: 9.43 us -> 13.7 us  [per_device(): lax.all_to_all(stale_keys[0], 'patch', split_axis=1, concat_axis=0, tiled...]
  transfers between devices with their start and end apart: 6 -> 8, of which waited for: 5 -> 6; matrix products, arithmetic and copies ran while one was open for 16% -> 26% of each run, Pallas kernels for 0% -> 0%
where the time goes in v1:
time: 259 us; the launch traced here: 258 us
  waiting for transfers between devices  128 us (49%)
  local copies, waits for them, and re-layouts  46.6 us (18%)
  matrix products  27.1 us (10%)
  between operations  16.3 us (6%)
  starting transfers between devices  15.1 us (6%)
  blocking collectives  13.6 us (5%)
  other arithmetic  11.5 us (4%)
    all_gather x1, waiting for transfers between devices, per_device(): lax.all_gather(out_weight, 'step', axis=0, tiled=True)  53.6 us
    ppermute x3, waiting for transfers between devices, define_the_core(): a_next = ppermute(a_next, comm_axis, perm=parts_out)  40 us
    unnamed x33, local copies, waits for them, and re-layouts  16.8 us
    all_to_all x1, waiting for transfers between devices, per_device(): lax.all_to_all(stale_keys[0], 'patch', split_axis=1, concat_axis=0, tiled...  13.7 us
    all_gather x1, blocking collectives, entering(): gathered = lax.all_gather(shard.astype(jnp.bfloat16), axis)  13.6 us
    all_to_all x1, waiting for transfers between devices, per_device(): lax.all_to_all(attended_every, 'patch', split_axis=0, concat_axis=1, tile...  10 us
    all_to_all x1, waiting for transfers between devices, per_device(): lax.all_to_all(stale_values[0], 'patch', split_axis=1, concat_axis=0, til...  9.92 us
    dot_general x1, matrix products, per_device(): jnp.dot(normed_every, lax.all_gather(query_columns, 'step', axis=0, tiled...  7.41 us
  transfers between devices with their start and end apart: 8, of which 6 were waited for; matrix products, arithmetic and copies ran while one was open for 26% of the time, Pallas kernels for 0%

profile of v1, /device:TPU:0, one launch (start us, length us, event | category | flops | bytes accessed | tf_op | source)
XLA Modules:
  0.0 258.1 jit_solution(17617583595388173476)
XLA Ops:
  11.9 3.1 %fusion.33 = f32[1,9216]{1,0:T(1,128)S(1)} fusion(bf16[256,1]{0,1:T(2,128)(2,1)S(1)} %reshape.107, bf16[256,9216]{1,0:T(8,128)(2,1)} %param.19), kind=kOutput, calls=%fused_computation.67 | convolution fusion | flops 4718592 | bytes 4755968 | tf_op jit(solution)/shard_map/dot_general | solution.py:134
  18.8 20.0 %collective-permute-done = bf16[256,3072]{1,0:T(8,128)(2,1)S(1)} collective-permute-done((bf16[256,3072]{1,0:T(8,128)(2,1)S(1)}, bf16[256,3072]{1,0:T(8,128)(2,1)S(1)}, u32[]{:S(2)}, u32[]{:S(2)}) %collective-permute-start) | collective-permute-done | bytes 1572896 | tf_op jit(solution)/shard_map/ppermute | solution.py:22
  40.0 19.9 %collective-permute-done.1 = bf16[256,3072]{1,0:T(8,128)(2,1)} collective-permute-done((bf16[256,3072]{1,0:T(8,128)(2,1)S(1)}, bf16[256,3072]{1,0:T(8,128)(2,1)}, u32[]{:S(2)}, u32[]{:S(2)}) %collective-permute-start.1) | collective-permute-done | bytes 1572896 | tf_op jit(solution)/shard_map/ppermute | solution.py:22
  64.9 4.2 %all-to-all-start = ((bf16[320,4,384]{2,0,1:T(8,128)(2,1)}), bf16[320,4,384]{2,0,1:T(8,128)(2,1)}, u32[]{:S(2)}, u32[]{:S(2)}) async-start(bf16[320,4,384]{2,0,1:T(8,128)(2,1)} %copy.38), calls=%async_computation | async-start | bytes 1966080 | tf_op jit(solution)/shard_map/all_to_all | solution.py:158
  69.1 2.7 %all_to_all.39 = bf16[320,4,384]{2,1,0:T(4,128)(2,1)} reshape(bf16[1,320,1536]{2,1,0:T(8,128)(2,1)} %param.25) | data formatting | bytes 1966080 | tf_op jit(solution)/shard_map/all_to_all | solution.py:159
  74.3 13.7 %all-to-all-done = bf16[320,4,384]{2,0,1:T(8,128)(2,1)} async-done(((bf16[320,4,384]{2,0,1:T(8,128)(2,1)}), bf16[320,4,384]{2,0,1:T(8,128)(2,1)}, u32[]{:S(2)}, u32[]{:S(2)}) %all-to-all-start) | async-done | bytes 983072 | tf_op jit(solution)/shard_map/all_to_all | solution.py:158
  88.0 5.9 %all-to-all-start.1 = ((bf16[320,4,384]{2,0,1:T(8,128)(2,1)}), bf16[320,4,384]{2,0,1:T(8,128)(2,1)}, u32[]{:S(2)}, u32[]{:S(2)}) async-start(bf16[320,4,384]{2,0,1:T(8,128)(2,1)} %copy.41), calls=%async_computation.1 | async-start | bytes 1966080 | tf_op jit(solution)/shard_map/all_to_all | solution.py:159
  93.9 3.7 %reshape.109 = bf16[1280,3,128]{2,1,0:T(4,128)(2,1)} reshape(bf16[4,320,384]{2,1,0:T(8,128)(2,1)} %bitcast.5) | data formatting | bytes 1966080 | tf_op jit(solution)/shard_map/reshape | solution.py:88
  97.6 9.9 %all-to-all-done.1 = bf16[320,4,384]{2,0,1:T(8,128)(2,1)} async-done(((bf16[320,4,384]{2,0,1:T(8,128)(2,1)}), bf16[320,4,384]{2,0,1:T(8,128)(2,1)}, u32[]{:S(2)}, u32[]{:S(2)}) %all-to-all-start.1) | async-done | bytes 983072 | tf_op jit(solution)/shard_map/all_to_all | solution.py:159
  107.5 3.7 %reshape.110 = bf16[1280,3,128]{2,1,0:T(4,128)(2,1)} reshape(bf16[4,320,384]{2,1,0:T(8,128)(2,1)} %bitcast.7) | data formatting | bytes 1966080 | tf_op jit(solution)/shard_map/reshape | solution.py:89
  111.2 2.8 %constant_dynamic-update-slice_fusion.7 = bf16[2048,3072]{1,0:T(8,128)(2,1)} fusion(bf16[256,3072]{1,0:T(8,128)(2,1)} %collective-permute-done.2), kind=kLoop, calls=%fused_computation.41 | loop fusion | bytes 3145728
  114.0 2.7 %constant_dynamic-update-slice_fusion.6 = bf16[2048,3072]{1,0:T(8,128)(2,1)} fusion(bf16[2048,3072]{1,0:T(8,128)(2,1)} %constant_dynamic-update-slice_fusion.7, bf16[256,3072]{1,0:T(8,128)(2,1)} %collective-permute-done.1), kind=kLoop, calls=%fused_computation.40 | loop fusion | bytes 3145728
  119.7 2.7 %constant_dynamic-update-slice_fusion.3 = bf16[2048,3072]{1,0:T(8,128)(2,1)} fusion(bf16[2048,3072]{1,0:T(8,128)(2,1)} %constant_dynamic-update-slice_fusion.4, bf16[256,3072]{1,0:T(8,128)(2,1)} %collective-permute-done.2), kind=kLoop, calls=%fused_computation.37 | loop fusion | bytes 3145728
  122.4 2.8 %constant_dynamic-update-slice_fusion.2 = bf16[2048,3072]{1,0:T(8,128)(2,1)} fusion(bf16[2048,3072]{1,0:T(8,128)(2,1)} %constant_dynamic-update-slice_fusion.3, bf16[256,3072]{1,0:T(8,128)(2,1)} %collective-permute-done.1), kind=kLoop, calls=%fused_computation.36 | loop fusion | bytes 3145728
  128.2 7.4 %fusion.6 = f32[1024,384]{0,1:T(8,128)} fusion(bf16[3072,384]{1,0:T(8,128)(2,1)} %all-gather.3.cloned.1.call-done, bf16[2048,3072]{1,0:T(8,128)(2,1)} %constant_dynamic-update-slice_fusion, s32[]{:T(128)S(6)} %select_n.29), kind=kOutput, calls=%fused_computation.8 | convolution fusion | flops 2415919104 | bytes 10223620 | tf_op jit(solution)/shard_map/dot_general | solution.py:151
  135.7 3.1 %copy.37 = f32[1024,3,128]{2,0,1:T(8,128)} copy(f32[1024,3,128]{0,2,1:T(8,128)} %bitcast.43) | data formatting | bytes 3145728 | tf_op jit(solution)/shard_map/reshape | solution.py:66
  140.4 4.3 %multiply_reduce_fusion = (f32[3,1024]{1,0:T(4,128)S(1)}, f32[3,1024,1280]{2,1,0:T(8,128)S(1)}) fusion(bf16[1280,3,128]{2,1,0:T(4,128)(2,1)} %reshape.109, f32[1024,3,128]{2,0,1:T(8,128)} %copy.37, f32[128]{0:T(128)S(1)} %copy-done.12, f32[1024,3]{0,1:T(4,128)S(1)} %add_rsqrt_fusion), kind=kOutput, calls=%fused_computation.2 | convolution fusion | flops 1015673856 | bytes 18309632 | tf_op jit(solution)/shard_map/qhd,khd->hqk/dot_general | solution.py:91
  144.7 3.3 %fusion = f32[3,1024]{1,0:T(4,128)S(1)} fusion(f32[3,1024,1280]{2,1,0:T(8,128)S(1)} %get-tuple-element.45, f32[3,1024]{1,0:T(4,128)S(1)} %get-tuple-element.44), kind=kLoop, calls=%fused_computation.3 | loop fusion | flops 11793408 | bytes 15753216 | tf_op jit(solution)/shard_map/reduce_sum | solution.py:97
  148.0 4.5 %fusion.11 = bf16[1024,3,128]{2,0,1:T(8,128)(2,1)} fusion(f32[3,1024,1280]{2,1,0:T(8,128)S(1)} %get-tuple-element.45, f32[3,1024]{1,0:T(4,128)S(1)} %get-tuple-element.44, bf16[1280,3,128]{2,1,0:T(4,128)(2,1)S(1)} %copy-done.4, f32[1024,3]{0,1:T(4,128)S(1)} %bitcast_add_fusion.1, f32[1024,3]{0,1:T(4,128)S(1)} %multiply_bitcast_fusion), kind=kOutput, calls=%fused_computation.20 | convolution fusion | flops 1019609088 | bytes 17534976 | tf_op jit(solution)/shard_map/hqk,khd->hqd/dot_general | solution.py:98
  159.6 4.4 %all-to-all-start.2 = ((bf16[4,256,384]{1,2,0:T(8,128)(2,1)}), bf16[4,256,384]{1,2,0:T(8,128)(2,1)}, u32[]{:S(2)}, u32[]{:S(2)}) async-start(bf16[4,256,384]{1,2,0:T(8,128)(2,1)} %copy.45), calls=%async_computation.2 | async-start | bytes 1572864 | tf_op jit(solution)/shard_map/all_to_all | solution.py:163
  165.4 10.0 %all-to-all-done.2 = bf16[4,256,384]{1,2,0:T(8,128)(2,1)} async-done(((bf16[4,256,384]{1,2,0:T(8,128)(2,1)}), bf16[4,256,384]{1,2,0:T(8,128)(2,1)}, u32[]{:S(2)}, u32[]{:S(2)}) %all-to-all-start.2) | async-done | bytes 786464 | tf_op jit(solution)/shard_map/all_to_all | solution.py:163
  175.5 53.6 %all-gather.5.cloned.1.call-done = bf16[3072,1536]{1,0:T(8,128)(2,1)} async-done(((bf16[768,1536]{1,0:T(8,128)(2,1)}), bf16[3072,1536]{1,0:T(8,128)(2,1)}) %all-gather.5.cloned.1.call-update) | async-done | bytes 9437200 | tf_op jit(solution)/shard_map/all_gather | solution.py:164
  229.1 5.6 %fusion.31 = (f32[256]{0:T(256)S(1)}, f32[256,3072]{1,0:T(8,128)S(1)}) fusion(f32[256,3072]{1,0:T(8,128)S(1)} %get-tuple-element.43, bf16[256,1536]{0,1:T(8,128)(2,1)} %bitcast.11, bf16[3072,1536]{1,0:T(8,128)(2,1)} %all-gather.5.cloned.1.call-done, f32[3072]{0:T(1024)S(1)} %copy-done.10), kind=kOutput, calls=%fused_computation.65 | convolution fusion | flops 2418278144 | bytes 16528384 | tf_op jit(solution)/shard_map/dot_general | solution.py:58
  236.6 13.6 %all_gather.12 = bf16[4,128,128]{2,1,0:T(8,128)(2,1)S(1)} all-gather(bf16[1,128,128]{2,1,0:T(8,128)(2,1)S(1)} %convert_element_type.62), channel_id=1, replica_groups=mesh['rep'=2,'step'=4,'patch'=4] {'step'}, dimensions={0}, use_global_device_ids=true | all-gather | bytes 163840 | tf_op jit(solution)/shard_map/all_gather | solution.py:32
  (75 shorter events, 34.2 us)
Async XLA Ops:
  6.5 1.7 copy-start
  6.5 4.0 %copy-start.11 = (f32[1000]{0:T(1024)S(1)}, f32[1000]{0:T(1024)}, u32[]{:S(2)}) copy-start(f32[1000]{0:T(1024)} %param.18) | copy-start | bytes 12004
  6.5 121.7 %all-gather.3.cloned.1.call-start = ((), (), s32[]{:S(2)}) async-start(), calls=%async_computation.3 | async-start | bytes 2949120 | tf_op jit(solution)/shard_map/all_gather | solution.py:153
  9.1 6.5 %copy-start.5 = (bf16[64,3072]{1,0:T(8,128)(2,1)S(1)}, bf16[64,3072]{1,0:T(8,128)(2,1)}, u32[]{:S(2)}) copy-start(bf16[64,3072]{1,0:T(8,128)(2,1)} %param.20) | copy-start | bytes 1179652
  9.1 220.0 %all-gather.5.cloned.1.call-start = ((), (), s32[]{:S(2)}) async-start(), calls=%async_computation.4 | async-start | bytes 11796480 | tf_op jit(solution)/shard_map/all_gather | solution.py:164
  15.6 2.0 copy-start.7
  18.3 20.6 %collective-permute-start = (bf16[256,3072]{1,0:T(8,128)(2,1)S(1)}, bf16[256,3072]{1,0:T(8,128)(2,1)S(1)}, u32[]{:S(2)}, u32[]{:S(2)}) collective-permute-start(bf16[256,3072]{1,0:T(8,128)(2,1)S(1)} %add_convert_fusion), channel_id=1, source_target_pairs={{0,1},{1,2},{2,3},{3,0},{4,5},{5,6},{6,7},{7,4},{8,9},{9,10},{10,1... | collective-permute-start | bytes 4718600 | tf_op jit(solution)/shard_map/ppermute | solution.py:22
  38.8 1.1 copy-start.2
  40.0 19.9 %collective-permute-start.1 = (bf16[256,3072]{1,0:T(8,128)(2,1)S(1)}, bf16[256,3072]{1,0:T(8,128)(2,1)}, u32[]{:S(2)}, u32[]{:S(2)}) collective-permute-start(bf16[256,3072]{1,0:T(8,128)(2,1)S(1)} %collective-permute-done), channel_id=1, source_target_pairs={{0,1},{1,2},{2,3},{3,0},{4,5},{5,6},{6,7},{7,4},{8,9},{9,10},{10,1... | collective-permute-start | bytes 4718600 | tf_op jit(solution)/shard_map/ppermute | solution.py:22
  59.9 51.3 %collective-permute-start.2 = (bf16[256,3072]{1,0:T(8,128)(2,1)}, bf16[256,3072]{1,0:T(8,128)(2,1)}, u32[]{:S(2)}, u32[]{:S(2)}) collective-permute-start(bf16[256,3072]{1,0:T(8,128)(2,1)} %collective-permute-done.1), channel_id=1, source_target_pairs={{0,1},{1,2},{2,3},{3,0},{4,5},{5,6},{6,7},{7,4},{8,9},{9,10},{10,1... | collective-permute-start | bytes 4718600 | tf_op jit(solution)/shard_map/ppermute | solution.py:22
  64.9 23.1 %all-to-all-start = ((bf16[320,4,384]{2,0,1:T(8,128)(2,1)}), bf16[320,4,384]{2,0,1:T(8,128)(2,1)}, u32[]{:S(2)}, u32[]{:S(2)}) async-start(bf16[320,4,384]{2,0,1:T(8,128)(2,1)} %copy.38), calls=%async_computation | async-start | bytes 1966080 | tf_op jit(solution)/shard_map/all_to_all | solution.py:158
  88.0 19.5 %all-to-all-start.1 = ((bf16[320,4,384]{2,0,1:T(8,128)(2,1)}), bf16[320,4,384]{2,0,1:T(8,128)(2,1)}, u32[]{:S(2)}, u32[]{:S(2)}) async-start(bf16[320,4,384]{2,0,1:T(8,128)(2,1)} %copy.41), calls=%async_computation.1 | async-start | bytes 1966080 | tf_op jit(solution)/shard_map/all_to_all | solution.py:159
  111.2 5.5 %copy-start.3 = (bf16[256,3072]{1,0:T(8,128)(2,1)S(1)}, bf16[256,3072]{1,0:T(8,128)(2,1)}, u32[]{:S(2)}) copy-start(bf16[256,3072]{1,0:T(8,128)(2,1)} %copy-done.2) | copy-start | bytes 4718596
  114.0 3.9 %copy-start.8 = (f32[3072]{0:T(1024)S(1)}, f32[3072]{0:T(1024)}, u32[]{:S(2)}) copy-start(f32[3072]{0:T(1024)} %copy-done.7) | copy-start | bytes 36868
  135.7 4.7 %copy-start.12 = (f32[128]{0:T(128)S(1)}, f32[128]{0:T(128)}, u32[]{:S(2)}) copy-start(f32[128]{0:T(128)} %param.23) | copy-start | bytes 1540
  144.6 3.4 %copy-start.4 = (bf16[1280,3,128]{2,1,0:T(4,128)(2,1)S(1)}, bf16[1280,3,128]{2,1,0:T(4,128)(2,1)}, u32[]{:S(2)}) copy-start(bf16[1280,3,128]{2,1,0:T(4,128)(2,1)} %reshape.110) | copy-start | bytes 2949124
  152.5 12.8 %copy-start.9 = (f32[256,64]{0,1:T(8,128)S(1)}, f32[256,64]{0,1:T(8,128)}, u32[]{:S(2)}) copy-start(f32[256,64]{0,1:T(8,128)} %param.16) | copy-start | bytes 196612
  152.5 76.6 %copy-start.10 = (f32[3072]{0:T(1024)S(1)}, f32[3072]{0:T(1024)}, u32[]{:S(2)}) copy-start(f32[3072]{0:T(1024)} %get-tuple-element.39) | copy-start | bytes 36868
  159.6 15.9 %all-to-all-start.2 = ((bf16[4,256,384]{1,2,0:T(8,128)(2,1)}), bf16[4,256,384]{1,2,0:T(8,128)(2,1)}, u32[]{:S(2)}, u32[]{:S(2)}) async-start(bf16[4,256,384]{1,2,0:T(8,128)(2,1)} %copy.45), calls=%async_computation.2 | async-start | bytes 1572864 | tf_op jit(solution)/shard_map/all_to_all | solution.py:163
  234.7 1.0 copy-start.6
  235.2 16.1 %copy-start.1 = (bf16[768,1536]{1,0:T(8,128)(2,1)S(1)}, bf16[768,1536]{1,0:T(8,128)(2,1)}, u32[]{:S(2)}) copy-start(bf16[768,1536]{1,0:T(8,128)(2,1)} %param.22) | copy-start | bytes 7077892
Sparse Core Ops, SparseCore 0:
  9.2 52.6 all-gather.2
  63.5 165.5 all-gather.4
